TPU v7x, 256 devices: a whole 4x4x8 slice. The times are simulated.
256 devices in a mesh: set: 8 (over y_hi, x), exp: 4 (over y_lo, core), seq: 8 (over z).
Axes of the slice: x: 4, y: 4 (y_hi: 2, y_lo: 2; y = y_hi * 2 + y_lo), z: 8, core: 2. Of those that a mesh axis runs over, the one named last changes fastest.
Arguments:
- tokens: bfloat16 [12288, 2560], P(('set', 'exp', 'seq')), parts along dimension 0, may hold values from -6 to 6
- expert_ids: int32 [12288, 2], P(('set', 'exp', 'seq')), parts along dimension 0, may hold values from 0 to 3, as said below
- gate_nums: int32 [12288, 2], P(('set', 'exp', 'seq')), parts along dimension 0, may hold values from 1 to 8
- moe_gain: float32 [2560], replicated, may hold values from 0.1 to 1.9
- w_gate_up: bfloat16 [4, 2560, 2, 3584], P('exp', None, None, 'seq'), may hold values from -0.125 to 0.125
- w_down: bfloat16 [4, 3584, 2560], P('exp', 'seq'), may hold values from -0.09375 to 0.09375
- attn_gain: float32 [2560], replicated, may hold values from 0.1 to 1.9
- w_qkv: bfloat16 [2560, 3, 2048], P(None, None, 'seq'), may hold values from -0.125 to 0.125
- q_gain: float32 [128], replicated, may hold values from 1.2 to 2.2
- k_gain: float32 [128], replicated, may hold values from 1.2 to 2.2
- w_out: bfloat16 [2048, 2560], P('seq'), may hold values from -0.125 to 0.125
Outputs:
- mixed: bfloat16 [12288, 2560], P(('set', 'exp', 'seq')), parts along dimension 0
- attended: bfloat16 [12288, 2560], P(('set', 'exp', 'seq')), parts along dimension 0
There are 8 independent parts, one for each index of `set`. A program takes and returns all parts, laid end to end along the dimension named above; an argument that names none is the same for every part. Nothing has to cross between parts.
Inputs may be any that keep to these rules, and one draw needn't show every extreme that they name: `expert_ids`: the two ids of a row differ. In the rows of one device no expert is named by more than 36 rows, and one expert, the same for all devices of a set, is named by exactly 36 of them.
All inputs are finite; a program needn't handle non-finite values.
Results may differ from a plain program's by a relative error of at most 0.014.
Values may be sent and summed in bfloat16 or wider, within the bound.
No kernel may reach another device: no remote copies, remote signals or barrier semaphores. Data moves between devices by JAX's collectives and lax.ppermute only.
A program may use at most 64 MiB of HBM per device.

v0:
```python
import math
import jax
import jax.numpy as jnp
from jax import lax
from jax.sharding import Mesh
from jax.sharding import PartitionSpec as P

EXPERTS = 4
CAP = 36
EXP = ("exp_0", "exp_1")
SET_EXP_SEQ = ("set", "exp_0", "exp_1", "seq")


def cut_along(value, dim, length):
    before, after = (value.shape[:dim], value.shape[dim + 1 :])
    return jnp.moveaxis(value.reshape(*before, length, -1, *after), dim, 0)


def joined_along(pieces, dim):
    lengths = list(pieces.shape[1:])
    lengths[dim] *= pieces.shape[0]
    return jnp.moveaxis(pieces, 0, dim).reshape(lengths)


def moved_by_axis(pieces, axes, order):
    inside = pieces.shape[1:]
    filled = pieces.reshape(*(lax.axis_size(a) for a in axes), *inside)
    for k in order:
        filled = lax.all_to_all(filled, axes[k], k, k, tiled=True)
    return filled.reshape(-1, *inside)


def two_step_exchange(value, groups, order, split_dim, concat_dim):
    length = lax.axis_size(groups[0]) * lax.axis_size(groups[1])
    pieces = cut_along(value, split_dim, length)
    return joined_along(moved_by_axis(pieces, groups, order), concat_dim)


def from_everyone(value, axis):
    length = lax.axis_size(axis)
    return lax.all_to_all(
        jnp.broadcast_to(value[None], (length, *value.shape)), axis, 0, 0, tiled=True
    )


def gather_directly(value, axis, dim):
    return joined_along(from_everyone(value, axis), dim)


def summed_on_arrival(value, axis, dim):
    length = lax.axis_size(axis)
    pieces = lax.all_to_all(cut_along(value, dim, length), axis, 0, 0, tiled=True)
    return jnp.sum(pieces.astype(jnp.float32), axis=0)


def rms_scale(values, gain):
    return values * lax.rsqrt(jnp.mean(values * values, axis=-1, keepdims=True) + 1e-06) * gain


def shards(
    tokens,
    expert_ids,
    gate_nums,
    moe_gain,
    w_gate_up,
    w_down,
    attn_gain,
    w_qkv,
    q_gain,
    k_gain,
    w_out,
):
    tok_rows = tokens.shape[0]
    model_dim = tokens.shape[1]
    tokens_wide = tokens.astype(jnp.float32)
    normed = rms_scale(tokens_wide, moe_gain).astype(jnp.bfloat16)
    flat_ids = expert_ids.reshape(-1)
    onehot = (flat_ids[:, None] == jnp.arange(EXPERTS)[None, :]).astype(jnp.int32)
    before = jnp.cumsum(onehot, axis=0) - onehot
    slot_index = jnp.sum(before * onehot, axis=1)
    destination = flat_ids * CAP + slot_index
    source_rows = normed[jnp.arange(2 * tok_rows) // 2]
    dispatch = jnp.zeros((EXPERTS * CAP, model_dim), jnp.bfloat16).at[destination].set(source_rows)
    dispatch = dispatch.reshape(EXPERTS, CAP, model_dim)
    received = two_step_exchange(dispatch, ("exp_0", "exp_1"), (1, 0), 0, 0)
    gate_up = jnp.einsum(
        "...d,dgf->...gf",
        lax.all_gather(received[None], "seq", axis=0, tiled=True),
        w_gate_up[0],
        preferred_element_type=jnp.float32,
    )
    hidden_all = (jax.nn.silu(gate_up[..., 0, :]) * gate_up[..., 1, :]).astype(jnp.bfloat16)
    summed = lax.psum_scatter(
        jnp.einsum(
            "...f,fd->...d", hidden_all, w_down[0], preferred_element_type=jnp.float32
        ).astype(jnp.bfloat16),
        "seq",
        scatter_dimension=0,
        tiled=True,
    ).astype(jnp.float32)
    expert_out = lax.all_to_all(
        summed[0].astype(jnp.bfloat16), EXP, split_axis=0, concat_axis=0, tiled=True
    ).astype(jnp.float32)
    picked = expert_out.reshape(EXPERTS * CAP, model_dim)[destination].reshape(
        tok_rows, 2, model_dim
    )
    nums = gate_nums.astype(jnp.float32)
    weights = nums / jnp.sum(nums, axis=1, keepdims=True)
    moe_total = jnp.sum(weights[:, :, None] * picked, axis=1)
    mixed = (tokens_wide + moe_total).astype(jnp.bfloat16)
    mixed_wide = mixed.astype(jnp.float32)
    attn_in = rms_scale(mixed_wide, attn_gain).astype(jnp.bfloat16)
    head_size = q_gain.shape[0]
    local_heads = w_qkv.shape[2] // head_size
    piece = gather_directly(attn_in, "seq", 0)
    qkv = jnp.einsum("nd,dgc->ngc", piece, w_qkv, preferred_element_type=jnp.float32)
    qkv = qkv.reshape(piece.shape[0], 3, local_heads, head_size)
    queries = rms_scale(qkv[:, 0], q_gain)
    keys_part = rms_scale(qkv[:, 1], k_gain)
    stacked = jnp.stack([queries, keys_part, qkv[:, 2]], axis=1)
    projected = stacked.reshape(piece.shape[0], 3, local_heads * head_size).astype(jnp.bfloat16)
    query_count = projected.shape[0]
    query_heads = projected[:, 0].reshape(query_count, local_heads, head_size)
    scale_factor = 1.0 / math.sqrt(head_size)
    key_piece = lax.all_gather(projected[:, 1], EXP, axis=0, tiled=True)
    value_piece = lax.all_gather(projected[:, 2], EXP, axis=0, tiled=True)
    key_heads = key_piece.reshape(key_piece.shape[0], local_heads, head_size)
    value_heads = value_piece.reshape(value_piece.shape[0], local_heads, head_size)
    scores = (
        jnp.einsum("qhc,khc->qhk", query_heads, key_heads, preferred_element_type=jnp.float32)
        * scale_factor
    )
    probs = jnp.exp(scores)
    denom = jnp.sum(probs, axis=-1)
    numer = jnp.einsum(
        "qhk,khc->qhc", probs.astype(jnp.bfloat16), value_heads, preferred_element_type=jnp.float32
    )
    numer, denom = (numer, denom)
    heads_out = (
        (numer / denom[:, :, None])
        .astype(jnp.bfloat16)
        .reshape(query_count, local_heads * head_size)
    )
    attn_rows = summed_on_arrival(
        jnp.dot(heads_out, w_out, preferred_element_type=jnp.float32).astype(jnp.bfloat16), "seq", 0
    )
    attended = (mixed_wide + attn_rows).astype(jnp.bfloat16)
    return (mixed, attended)


def solution(mesh):
    torus = Mesh(
        mesh.devices.reshape(mesh.shape["set"], 2, 2, mesh.shape["seq"]),
        ("set", "exp_0", "exp_1", "seq"),
    )
    in_specs = (
        P(SET_EXP_SEQ, None),
        P(SET_EXP_SEQ, None),
        P(SET_EXP_SEQ, None),
        P(),
        P(EXP, None, None, "seq"),
        P(EXP, "seq", None),
        P(),
        P(None, None, "seq"),
        P(),
        P(),
        P("seq", None),
    )
    out_specs = (P(SET_EXP_SEQ, None), P(SET_EXP_SEQ, None))
    return jax.shard_map(
        shards, mesh=torus, in_specs=in_specs, out_specs=out_specs, check_vma=False
    )
```

profile of v0, /device:TPU:1, one launch (start us, length us, event | category | flops | bytes accessed | tf_op | source)
XLA Modules:
  0.0 367.5 jit_solution(4428204008842671317)
XLA Ops:
  7.2 0.9 copy.38
  8.1 0.7 broadcast_multiply_fusion
  8.8 0.1 eq.15
  9.0 0.1 fusion.28
  9.0 0.1 reduce_window_sum.11
  9.2 0.2 select_reduce_fusion
  9.4 0.1 copy.37
  9.5 0.1 mul.128
  9.6 1.1 fusion.12
  10.7 1.1 fusion.14
  11.8 3.7 %scatter_custom_fusion = bf16[144,2560]{1,0:T(8,128)(2,1)} fusion(s32[96]{0:T(128)S(1)} %fusion.30, bf16[48,2560]{1,0:T(8,128)(2,1)S(1)} %fusion.14, s32[1024]{0:T(1024)S(1)} %pad_clamp_fusion.1, bf16[]{:T(256)} %constant.36.clone.1), kind=kCustom, calls=%fused_computation.36 | custom fusion | bytes 737282 | tf_op jit(solution)/shard_map/scatter | solution.py:83
  15.5 1.3 reshape_reshape_reshape.3
  16.8 0.8 copy.39
  17.5 7.1 %all_to_all.25 = bf16[2,2,1,36,2560]{4,0,3,2,1:T(2,128)(2,1)S(1)} all-to-all(bf16[2,2,1,36,2560]{4,0,3,2,1:T(2,128)(2,1)S(1)} %copy.39), channel_id=1, replica_groups=mesh['set'=8,'exp_0'=2,'exp_1'=2,'seq'=8] {'exp_1'}, dimensions={1} | all-to-all | bytes 1474560 | tf_op jit(solution)/shard_map/all_to_all | solution.py:29
  24.7 0.6 copy.40
  25.2 12.4 %all_to_all.26 = bf16[2,2,1,36,2560]{4,1,3,2,0:T(2,128)(2,1)S(1)} all-to-all(bf16[2,2,1,36,2560]{4,1,3,2,0:T(2,128)(2,1)S(1)} %copy.40), channel_id=1, replica_groups=mesh['set'=8,'exp_0'=2,'exp_1'=2,'seq'=8] {'exp_0'}, dimensions={0} | all-to-all | bytes 1474560 | tf_op jit(solution)/shard_map/all_to_all | solution.py:29
  37.6 0.5 copy.41
  38.1 1.2 broadcast_in_dim_reshape_reshape.3
  39.3 0.0 reduce-scatter.2.cloned.1.call-start
  39.4 72.5 %all-gather.2.cloned.1.call-done = bf16[8,4,36,2560]{3,1,2,0:T(4,128)(2,1)} async-done(((bf16[1,4,36,2560]{3,1,2,0:T(4,128)(2,1)}), bf16[8,4,36,2560]{3,1,2,0:T(4,128)(2,1)}) %all-gather.2.cloned.1.call-update) | async-done | bytes 5898256 | tf_op jit(solution)/shard_map/all_gather | solution.py:88
  111.9 10.4 %fusion = f32[8,4,36,2,448]{4,2,3,1,0:T(8,128)S(1)} fusion(bf16[8,4,36,2560,1]{3,1,2,0,4:T(4,128)(2,1)} %bitcast.78, bf16[1,2560,2,448]{1,3,2,0:T(8,128)(2,1)} %param.15), kind=kOutput, calls=%fused_computation.3 | convolution fusion | flops 5284823040 | bytes 14614528 | tf_op jit(solution)/shard_map/...d,dgf->...gf/dot_general | solution.py:86
  122.2 5.7 %convolution_convert_fusion = bf16[8,4,36,2560]{3,2,1,0:T(8,128)(2,1)} fusion(bf16[1,448,2560]{2,1,0:T(8,128)(2,1)S(1)} %copy-done, f32[8,4,36,2,448]{4,2,3,1,0:T(8,128)S(1)} %fusion), kind=kOutput, calls=%fused_computation.5 | convolution fusion | flops 2648457216 | bytes 12320768 | tf_op jit(solution)/shard_map/...f,fd->...d/dot_general | solution.py:94
  127.9 76.4 %reduce-scatter.2.cloned.1.call-done = bf16[1,4,36,2560]{3,2,1,0:T(8,128)(2,1)} async-done(((bf16[8,4,36,2560]{3,2,1,0:T(8,128)(2,1)}), bf16[1,4,36,2560]{3,2,1,0:T(8,128)(2,1)}) %reduce-scatter.2.cloned.1.call-update) | async-done | bytes 737296 | tf_op jit(solution)/shard_map/reduce_scatter | solution.py:93
  204.4 4.2 %all-to-all-start.2 = ((bf16[4,36,2560]{2,1,0:T(8,128)(2,1)}), bf16[4,36,2560]{2,1,0:T(8,128)(2,1)S(1)}, u32[]{:S(2)}, u32[]{:S(2)}) async-start(bf16[4,36,2560]{2,1,0:T(8,128)(2,1)} %bitcast.75), calls=%async_computation.3 | async-start | bytes 1638400 | tf_op jit(solution)/shard_map/all_to_all | solution.py:101
  208.6 0.1 copy.36
  208.7 10.9 %all-to-all-done.2 = bf16[4,36,2560]{2,1,0:T(8,128)(2,1)S(1)} async-done(((bf16[4,36,2560]{2,1,0:T(8,128)(2,1)}), bf16[4,36,2560]{2,1,0:T(8,128)(2,1)S(1)}, u32[]{:S(2)}, u32[]{:S(2)}) %all-to-all-start.2) | async-done | bytes 737312 | tf_op jit(solution)/shard_map/all_to_all | solution.py:101
  219.6 1.3 reshape.166
  220.9 2.7 gather_fusion
  223.6 1.5 reshape.159
  225.2 2.6 multiply_reduce_fusion
  227.7 0.2 fusion.16
  227.9 0.9 fusion.18
  228.8 1.4 broadcast_in_dim.5
  230.3 4.3 %all-to-all-start.3 = ((bf16[8,48,2560]{2,1,0:T(8,128)(2,1)}), bf16[8,48,2560]{2,1,0:T(8,128)(2,1)}, u32[]{:S(2)}, u32[]{:S(2)}) async-start(bf16[8,48,2560]{2,1,0:T(8,128)(2,1)} %broadcast_in_dim.5), calls=%async_computation.4 | async-start | bytes 3932160 | tf_op jit(solution)/shard_map/all_to_all | solution.py:41
  234.6 6.3 %copy.56 = bf16[3,256,2560]{2,1,0:T(8,128)(2,1)} copy(bf16[3,256,2560]{1,2,0:T(8,128)(2,1)} %bitcast.70) | data formatting | bytes 7864320 | tf_op jit(solution)/shard_map/nd,dgc->ngc/dot_general | solution.py:116
  240.9 39.4 %all-to-all-done.3 = bf16[8,48,2560]{2,1,0:T(8,128)(2,1)} async-done(((bf16[8,48,2560]{2,1,0:T(8,128)(2,1)}), bf16[8,48,2560]{2,1,0:T(8,128)(2,1)}, u32[]{:S(2)}, u32[]{:S(2)}) %all-to-all-start.3) | async-done | bytes 1966112 | tf_op jit(solution)/shard_map/all_to_all | solution.py:41
  280.3 4.9 %fusion.34 = f32[384,3,2,128]{0,3,2,1:T(8,128)S(1)} fusion(bf16[384,2560,1,1]{1,0,3,2:T(8,128)(2,1)} %bitcast.14, bf16[3,2,128,2560]{3,2,1,0:T(8,128)(2,1)} %bitcast.71), kind=kOutput, calls=%fused_computation.71 | convolution fusion | flops 1509949440 | bytes 7077888 | tf_op jit(solution)/shard_map/nd,dgc->ngc/dot_general | solution.py:116
  285.2 0.1 multiply_reduce_fusion.1
  285.3 0.1 multiply_convert_fusion.1
  285.4 11.2 %all_gather.11 = bf16[1536,256]{0,1:T(8,128)(2,1)S(1)} all-gather(bf16[384,256]{0,1:T(8,128)(2,1)S(1)} %bitcast.77), channel_id=1, replica_groups=mesh['set'=8,'exp_0'=2,'exp_1'=2,'seq'=8] {'exp_0','exp_1'}, dimensions={0}, use_global_device_ids=true | all-gather | bytes 983040 | tf_op jit(solution)/shard_map/all_gather | solution.py:125
  296.7 8.7 %all_gather.10 = bf16[1536,256]{0,1:T(8,128)(2,1)S(1)} all-gather(bf16[384,256]{0,1:T(8,128)(2,1)S(1)} %bitcast.76), channel_id=1, replica_groups=mesh['set'=8,'exp_0'=2,'exp_1'=2,'seq'=8] {'exp_0','exp_1'}, dimensions={0}, use_global_device_ids=true | all-gather | bytes 983040 | tf_op jit(solution)/shard_map/all_gather | solution.py:126
  305.4 1.0 bitcast_reduce_fusion
  306.3 0.8 fusion.11
  307.2 0.5 copy-done.3
  307.7 0.7 convolution_convert_fusion.1
  308.3 51.3 %all_to_all.27 = bf16[8,48,2560]{2,1,0:T(8,128)(2,1)S(1)} all-to-all(bf16[8,48,2560]{2,1,0:T(8,128)(2,1)S(1)} %bitcast.69), channel_id=1, replica_groups=mesh['set'=8,'exp_0'=2,'exp_1'=2,'seq'=8] {'seq'}, dimensions={0} | all-to-all | bytes 3932160 | tf_op jit(solution)/shard_map/all_to_all | solution.py:52
  359.7 0.3 convert_reduce_fusion
  359.9 0.8 fusion.19
  (27 shorter events, 0.2 us)
Async XLA Ops:
  7.2 115.1 %copy-start = (bf16[1,448,2560]{2,1,0:T(8,128)(2,1)S(1)}, bf16[1,448,2560]{2,1,0:T(8,128)(2,1)}, u32[]{:S(2)}) copy-start(bf16[1,448,2560]{2,1,0:T(8,128)(2,1)} %param.16) | copy-start | bytes 6881284
  7.2 104.7 %all-gather.2.cloned.1.call-start = ((), (), s32[]{:S(2)}) async-start(), calls=%async_computation.6 | async-start | bytes 6635520 | tf_op jit(solution)/shard_map/all_gather | solution.py:88
  39.3 165.1 %reduce-scatter.2.cloned.1.call-start = ((), (), s32[]{:S(2)}) async-start(), calls=%async_computation.7 | async-start | bytes 7372800 | tf_op jit(solution)/shard_map/reduce_scatter | solution.py:93
  127.9 80.7 %copy-start.4 = (s32[48,2]{0,1:T(2,128)S(1)}, s32[48,2]{0,1:T(2,128)}, u32[]{:S(2)}) copy-start(s32[48,2]{0,1:T(2,128)} %param.13) | copy-start | bytes 1156
  204.4 15.2 %all-to-all-start.2 = ((bf16[4,36,2560]{2,1,0:T(8,128)(2,1)}), bf16[4,36,2560]{2,1,0:T(8,128)(2,1)S(1)}, u32[]{:S(2)}, u32[]{:S(2)}) async-start(bf16[4,36,2560]{2,1,0:T(8,128)(2,1)} %bitcast.75), calls=%async_computation.3 | async-start | bytes 1638400 | tf_op jit(solution)/shard_map/all_to_all | solution.py:101
  223.6 4.1 %copy-start.1 = (bf16[48,2560]{1,0:T(8,128)(2,1)S(1)}, bf16[48,2560]{1,0:T(8,128)(2,1)}, u32[]{:S(2)}) copy-start(bf16[48,2560]{1,0:T(8,128)(2,1)} %param.11) | copy-start | bytes 737284
  227.9 132.0 %copy-start.2 = (bf16[48,2560]{1,0:T(8,128)(2,1)}, bf16[48,2560]{1,0:T(8,128)(2,1)S(1)}, u32[]{:S(2)}) copy-start(bf16[48,2560]{1,0:T(8,128)(2,1)S(1)} %get-tuple-element.5) | copy-start | bytes 737284
  230.3 50.0 %all-to-all-start.3 = ((bf16[8,48,2560]{2,1,0:T(8,128)(2,1)}), bf16[8,48,2560]{2,1,0:T(8,128)(2,1)}, u32[]{:S(2)}, u32[]{:S(2)}) async-start(bf16[8,48,2560]{2,1,0:T(8,128)(2,1)} %broadcast_in_dim.5), calls=%async_computation.4 | async-start | bytes 3932160 | tf_op jit(solution)/shard_map/all_to_all | solution.py:41
  280.3 5.1 %copy-start.6 = (f32[128]{0:T(128)S(1)}, f32[128]{0:T(128)}, u32[]{:S(2)}) copy-start(f32[128]{0:T(128)} %param.20) | copy-start | bytes 1540
  285.2 20.2 %copy-start.5 = (f32[128]{0:T(128)S(1)}, f32[128]{0:T(128)}, u32[]{:S(2)}) copy-start(f32[128]{0:T(128)} %param.19) | copy-start | bytes 1540
  306.3 1.3 copy-start.3
Sparse Core Ops, SparseCore 0:
  39.4 72.3 all-gather.1
  128.1 76.2 reduce-scatter.1
where the time goes:
time: 368 us
  waiting for transfers between devices  199 us (54%)
  blocking collectives  90.7 us (25%)
  matrix products  23.4 us (6%)
  local copies, waits for them, and re-layouts  23.1 us (6%)
  between operations  14.3 us (4%)
  starting transfers between devices  8.64 us (2%)
  other arithmetic  8.14 us (2%)
    reduce_scatter x1, waiting for transfers between devices, shards(): lax.psum_scatter(jnp.einsum('...f,fd->...d', hidden_all, w_down[0], prefe...  76.4 us
    all_gather x1, waiting for transfers between devices, shards(): lax.all_gather(received[None], 'seq', axis=0, tiled=True)  72.5 us
    all_to_all x1, blocking collectives, summed_on_arrival(): lax.all_to_all(cut_along(value, dim, length), axis, 0, 0, tiled=True)  51.3 us
    all_to_all x1, waiting for transfers between devices, from_everyone(): lax.all_to_all(jnp.broadcast_to(value[None], (length, *value.shape)), axi...  39.4 us
    all_to_all x2, blocking collectives, moved_by_axis(): filled = lax.all_to_all(filled, axes[k], k, k, tiled=True)  19.5 us
    all_gather x1, blocking collectives, shards(): key_piece = lax.all_gather(projected[:, 1], EXP, axis=0, tiled=True)  11.2 us
    all_to_all x1, waiting for transfers between devices, shards(): lax.all_to_all(summed[0].astype(jnp.bfloat16), EXP, split_axis=0, concat_...  10.9 us
    dot_general x1, matrix products, shards(): jnp.einsum('...d,dgf->...gf', lax.all_gather(received[None], 'seq', axis=...  10.4 us
  transfers between devices with their start and end apart: 4, of which 4 were waited for; matrix products, arithmetic and copies ran while one was open for 2% of the time, Pallas kernels for 0%

commit v1 on v0

--- a/solution.py
+++ b/solution.py
@@ -70,6 +70,13 @@
     k_gain,
     w_out,
 ):
+
+    def regions_resolve(vec, out_dim):
+        left_arr = jnp.concatenate(
+            lax.all_to_all(jnp.stack(lax.axis_size("seq") * [vec], 0), "seq", 0, 0), out_dim
+        )
+        return left_arr
+
     tok_rows = tokens.shape[0]
     model_dim = tokens.shape[1]
     tokens_wide = tokens.astype(jnp.float32)
@@ -85,7 +92,7 @@
     received = two_step_exchange(dispatch, ("exp_0", "exp_1"), (1, 0), 0, 0)
     gate_up = jnp.einsum(
         "...d,dgf->...gf",
-        lax.all_gather(received[None], "seq", axis=0, tiled=True),
+        regions_resolve(received[None], 0),
         w_gate_up[0],
         preferred_element_type=jnp.float32,
     )

time: 368 us -> 427 us (1.16)
  blocking collectives: 90.7 us -> 225 us
  waiting for transfers between devices: 199 us -> 130 us
    all_to_all x0 -> x1, blocking collectives: none -> 137 us  [regions_resolve(): lax.all_to_all(jnp.stack(lax.axis_size('seq') * [vec], 0), 'seq', 0, 0)]
    all_gather x1 -> x0, waiting for transfers between devices: 72.5 us -> none  [shards(): lax.all_gather(received[None], 'seq', axis=0, tiled=True)]
  transfers between devices with their start and end apart: 4 -> 3, of which waited for: 4 -> 3; matrix products, arithmetic and copies ran while one was open for 2% -> 1% of each run, Pallas kernels for 0% -> 0%
where the time goes in v1:
time: 427 us; the launch traced here: 426 us
  blocking collectives  225 us (53%)
  waiting for transfers between devices  130 us (30%)
  local copies, waits for them, and re-layouts  22.8 us (5%)
  matrix products  19.6 us (5%)
  between operations  14.3 us (3%)
  starting transfers between devices  8.31 us (2%)
  other arithmetic  6.16 us (1%)
    all_to_all x1, blocking collectives, regions_resolve(): lax.all_to_all(jnp.stack(lax.axis_size('seq') * [vec], 0), 'seq', 0, 0)  137 us
    reduce_scatter x1, waiting for transfers between devices, shards(): lax.psum_scatter(jnp.einsum('...f,fd->...d', hidden_all, w_down[0], prefe...  76.7 us
    all_to_all x1, blocking collectives, summed_on_arrival(): lax.all_to_all(cut_along(value, dim, length), axis, 0, 0, tiled=True)  51.4 us
    all_to_all x1, waiting for transfers between devices, from_everyone(): lax.all_to_all(jnp.broadcast_to(value[None], (length, *value.shape)), axi...  42.6 us
    all_to_all x2, blocking collectives, moved_by_axis(): filled = lax.all_to_all(filled, axes[k], k, k, tiled=True)  19.5 us
    all_to_all x1, waiting for transfers between devices, shards(): lax.all_to_all(summed[0].astype(jnp.bfloat16), EXP, split_axis=0, concat_...  10.9 us
    all_gather x1, blocking collectives, shards(): key_piece = lax.all_gather(projected[:, 1], EXP, axis=0, tiled=True)  8.71 us
    all_gather x1, blocking collectives, shards(): value_piece = lax.all_gather(projected[:, 2], EXP, axis=0, tiled=True)  8.7 us
  transfers between devices with their start and end apart: 3, of which 3 were waited for; matrix products, arithmetic and copies ran while one was open for 1% of the time, Pallas kernels for 0%

profile of v1, /device:TPU:1, one launch (start us, length us, event | category | flops | bytes accessed | tf_op | source)
XLA Modules:
  0.0 426.5 jit_solution(8484641740254395847)
XLA Ops:
  7.2 0.9 copy.38
  8.1 0.7 broadcast_multiply_fusion
  8.8 0.1 eq.15
  9.0 0.1 fusion.29
  9.0 0.1 reduce_window_sum.11
  9.2 0.2 select_reduce_fusion
  9.4 0.1 copy.37
  9.5 0.1 mul.128
  9.6 1.1 fusion.13
  10.7 1.1 fusion.15
  11.8 3.7 scatter_custom_fusion
  15.5 1.3 reshape_reshape_reshape.3
  16.8 0.8 copy.39
  17.5 7.1 %all_to_all.30 = bf16[2,2,1,36,2560]{4,0,3,2,1:T(2,128)(2,1)S(1)} all-to-all(bf16[2,2,1,36,2560]{4,0,3,2,1:T(2,128)(2,1)S(1)} %copy.39), channel_id=1, replica_groups=mesh['set'=8,'exp_0'=2,'exp_1'=2,'seq'=8] {'exp_1'}, dimensions={1} | all-to-all | bytes 1474560 | tf_op jit(solution)/shard_map/all_to_all | solution.py:29
  24.7 0.6 copy.40
  25.2 12.4 %all_to_all.31 = bf16[2,2,1,36,2560]{4,1,3,2,0:T(2,128)(2,1)S(1)} all-to-all(bf16[2,2,1,36,2560]{4,1,3,2,0:T(2,128)(2,1)S(1)} %copy.40), channel_id=1, replica_groups=mesh['set'=8,'exp_0'=2,'exp_1'=2,'seq'=8] {'exp_0'}, dimensions={0} | all-to-all | bytes 1474560 | tf_op jit(solution)/shard_map/all_to_all | solution.py:29
  37.6 1.4 copy.41
  39.0 2.4 stack_broadcast_in_dim_reshape_reshape.2
  41.4 1.5 stack.2
  42.9 136.7 %all_to_all.32 = bf16[8,1,4,36,2560]{4,2,3,1,0:T(4,128)(2,1)S(1)} all-to-all(bf16[8,1,4,36,2560]{4,2,3,1,0:T(4,128)(2,1)S(1)} %stack.2), channel_id=1, replica_groups=mesh['set'=8,'exp_0'=2,'exp_1'=2,'seq'=8] {'seq'}, dimensions={0} | all-to-all | bytes 11796480 | tf_op jit(solution)/shard_map/all_to_all | solution.py:76
  179.6 7.1 %fusion = f32[8,4,36,2,448]{4,2,3,1,0:T(8,128)S(1)} fusion(bf16[8,1,4,36,2560]{4,2,3,1,0:T(4,128)(2,1)S(1)} %all_to_all.32, bf16[1,2560,2,448]{1,3,2,0:T(8,128)(2,1)S(1)} %bitcast.85), kind=kOutput, calls=%fused_computation.3 | convolution fusion | flops 5284823040 | bytes 14614528 | tf_op jit(solution)/shard_map/...d,dgf->...gf/dot_general | solution.py:93
  186.8 5.7 %convolution_convert_fusion = bf16[8,4,36,2560]{3,2,1,0:T(8,128)(2,1)} fusion(bf16[1,448,2560]{2,1,0:T(8,128)(2,1)S(1)} %copy-done, f32[8,4,36,2,448]{4,2,3,1,0:T(8,128)S(1)} %fusion), kind=kOutput, calls=%fused_computation.6 | convolution fusion | flops 2648457216 | bytes 12320768 | tf_op jit(solution)/shard_map/...f,fd->...d/dot_general | solution.py:101
  192.5 76.7 %reduce-scatter.2.cloned.1.call-done = bf16[1,4,36,2560]{3,2,1,0:T(8,128)(2,1)} async-done(((bf16[8,4,36,2560]{3,2,1,0:T(8,128)(2,1)}), bf16[1,4,36,2560]{3,2,1,0:T(8,128)(2,1)}) %reduce-scatter.2.cloned.1.call-update) | async-done | bytes 737296 | tf_op jit(solution)/shard_map/reduce_scatter | solution.py:100
  269.2 4.2 all-to-all-start.3
  273.4 0.1 copy.36
  273.5 10.9 %all-to-all-done.3 = bf16[4,36,2560]{2,1,0:T(8,128)(2,1)S(1)} async-done(((bf16[4,36,2560]{2,1,0:T(8,128)(2,1)}), bf16[4,36,2560]{2,1,0:T(8,128)(2,1)S(1)}, u32[]{:S(2)}, u32[]{:S(2)}) %all-to-all-start.3) | async-done | bytes 737312 | tf_op jit(solution)/shard_map/all_to_all | solution.py:108
  284.4 0.1 reshape.174
  284.5 0.9 gather_fusion
  285.5 0.6 reshape.167
  286.1 1.3 multiply_reduce_fusion
  287.4 0.2 fusion.17
  287.6 0.1 fusion.19
  287.7 1.5 broadcast_in_dim.5
  289.2 4.1 all-to-all-start.4
  293.3 6.2 %copy.54 = bf16[3,256,2560]{2,1,0:T(8,128)(2,1)} copy(bf16[3,256,2560]{1,2,0:T(8,128)(2,1)} %bitcast.75) | data formatting | bytes 7864320 | tf_op jit(solution)/shard_map/nd,dgc->ngc/dot_general | solution.py:123
  299.5 42.6 %all-to-all-done.4 = bf16[8,48,2560]{2,1,0:T(8,128)(2,1)S(1)} async-done(((bf16[8,48,2560]{2,1,0:T(8,128)(2,1)}), bf16[8,48,2560]{2,1,0:T(8,128)(2,1)S(1)}, u32[]{:S(2)}, u32[]{:S(2)}) %all-to-all-start.4) | async-done | bytes 1966112 | tf_op jit(solution)/shard_map/all_to_all | solution.py:41
  342.1 4.3 %fusion.35 = f32[384,3,2,128]{0,3,2,1:T(8,128)S(1)} fusion(bf16[384,2560,1,1]{1,0,3,2:T(8,128)(2,1)S(1)} %bitcast.79, bf16[3,2,128,2560]{3,2,1,0:T(8,128)(2,1)} %bitcast.76), kind=kOutput, calls=%fused_computation.72 | convolution fusion | flops 1509949440 | bytes 7077888 | tf_op jit(solution)/shard_map/nd,dgc->ngc/dot_general | solution.py:123
  346.5 0.1 multiply_reduce_fusion.1
  346.6 0.1 multiply_convert_fusion.1
  346.7 8.7 %all_gather.7 = bf16[1536,256]{0,1:T(8,128)(2,1)S(1)} all-gather(bf16[384,256]{0,1:T(8,128)(2,1)S(1)} %bitcast.83), channel_id=1, replica_groups=mesh['set'=8,'exp_0'=2,'exp_1'=2,'seq'=8] {'exp_0','exp_1'}, dimensions={0}, use_global_device_ids=true | all-gather | bytes 983040 | tf_op jit(solution)/shard_map/all_gather | solution.py:132
  355.4 8.7 %all_gather.6 = bf16[1536,256]{0,1:T(8,128)(2,1)S(1)} all-gather(bf16[384,256]{0,1:T(8,128)(2,1)S(1)} %bitcast.82), channel_id=1, replica_groups=mesh['set'=8,'exp_0'=2,'exp_1'=2,'seq'=8] {'exp_0','exp_1'}, dimensions={0}, use_global_device_ids=true | all-gather | bytes 983040 | tf_op jit(solution)/shard_map/all_gather | solution.py:133
  364.1 1.0 bitcast_reduce_fusion
  365.1 0.8 fusion.12
  365.9 0.5 copy-done.4
  366.4 0.7 convolution_convert_fusion.1
  367.1 51.4 %all_to_all.33 = bf16[8,48,2560]{2,1,0:T(8,128)(2,1)S(1)} all-to-all(bf16[8,48,2560]{2,1,0:T(8,128)(2,1)S(1)} %bitcast.74), channel_id=1, replica_groups=mesh['set'=8,'exp_0'=2,'exp_1'=2,'seq'=8] {'seq'}, dimensions={0} | all-to-all | bytes 3932160 | tf_op jit(solution)/shard_map/all_to_all | solution.py:52
  418.6 0.3 convert_reduce_fusion
  418.9 0.8 fusion.20
  (35 shorter events, 0.2 us)
Async XLA Ops:
  7.2 179.6 %copy-start = (bf16[1,448,2560]{2,1,0:T(8,128)(2,1)S(1)}, bf16[1,448,2560]{2,1,0:T(8,128)(2,1)}, u32[]{:S(2)}) copy-start(bf16[1,448,2560]{2,1,0:T(8,128)(2,1)} %param.16) | copy-start | bytes 6881284
  7.2 262.0 %reduce-scatter.2.cloned.1.call-start = ((), (), s32[]{:S(2)}) async-start(), calls=%async_computation.7 | async-start | bytes 7372800 | tf_op jit(solution)/shard_map/reduce_scatter | solution.py:100
  41.4 138.3 %slice-start = ((s8[4587520]{0:T(1024)(128)(4,1)}), s8[4194304]{0:T(1024)(128)(4,1)S(1)}, s32[]{:S(2)}) async-start(s8[4587520]{0:T(1024)(128)(4,1)} %bitcast.84), calls=%async_computation.8 | async-start | bytes 8388608
  42.9 136.7 %slice-start.1 = ((s8[4587520]{0:T(1024)(128)(4,1)}), s8[393216]{0:T(1024)(128)(4,1)S(1)}, s32[]{:S(2)}) async-start(s8[4587520]{0:T(1024)(128)(4,1)} %bitcast.84), calls=%async_computation.9 | async-start | bytes 786432
  192.4 80.9 %copy-start.6 = (s32[48,2]{0,1:T(2,128)S(1)}, s32[48,2]{0,1:T(2,128)}, u32[]{:S(2)}) copy-start(s32[48,2]{0,1:T(2,128)} %param.13) | copy-start | bytes 1156
  269.2 15.2 %all-to-all-start.3 = ((bf16[4,36,2560]{2,1,0:T(8,128)(2,1)}), bf16[4,36,2560]{2,1,0:T(8,128)(2,1)S(1)}, u32[]{:S(2)}, u32[]{:S(2)}) async-start(bf16[4,36,2560]{2,1,0:T(8,128)(2,1)} %bitcast.81), calls=%async_computation.4 | async-start | bytes 1638400 | tf_op jit(solution)/shard_map/all_to_all | solution.py:108
  285.4 1.9 copy-start.2
  285.5 2.1 copy-start.5
  287.6 131.3 %copy-start.3 = (bf16[48,2560]{1,0:T(8,128)(2,1)}, bf16[48,2560]{1,0:T(8,128)(2,1)S(1)}, u32[]{:S(2)}) copy-start(bf16[48,2560]{1,0:T(8,128)(2,1)S(1)} %get-tuple-element.5) | copy-start | bytes 737284
  289.2 52.9 %all-to-all-start.4 = ((bf16[8,48,2560]{2,1,0:T(8,128)(2,1)}), bf16[8,48,2560]{2,1,0:T(8,128)(2,1)S(1)}, u32[]{:S(2)}, u32[]{:S(2)}) async-start(bf16[8,48,2560]{2,1,0:T(8,128)(2,1)} %broadcast_in_dim.5), calls=%async_computation.5 | async-start | bytes 3932160 | tf_op jit(solution)/shard_map/all_to_all | solution.py:41
  342.1 4.5 %copy-start.8 = (f32[128]{0:T(128)S(1)}, f32[128]{0:T(128)}, u32[]{:S(2)}) copy-start(f32[128]{0:T(128)} %param.20) | copy-start | bytes 1540
  346.5 17.7 %copy-start.7 = (f32[128]{0:T(128)S(1)}, f32[128]{0:T(128)}, u32[]{:S(2)}) copy-start(f32[128]{0:T(128)} %param.19) | copy-start | bytes 1540
  365.1 1.3 copy-start.4
  367.1 52.5 %copy-start.1 = (bf16[1,448,2560]{2,1,0:T(8,128)(2,1)S(1)}, bf16[1,448,2560]{2,1,0:T(8,128)(2,1)}, u32[]{:S(2)}) copy-start(bf16[1,448,2560]{2,1,0:T(8,128)(2,1)} %param.16) | copy-start | bytes 6881284
Sparse Core Ops, SparseCore 0:
  192.6 76.5 reduce-scatter.1
